TPU v7x, 32 devices: a whole 2x2x4 slice. The times are simulated.
32 devices in a mesh: cells: 8 (over y, x, core), modes: 4 (over z).
Axes of the slice: x: 2, y: 2, z: 4, core: 2. Of those that a mesh axis runs over, the one named last changes fastest.
Arguments:
- phonons: float32 [8, 8, 8, 16, 6144], P('cells', None, None, None, 'modes'), may hold values from -6 to 6
- heaters: int32 [8, 8, 8, 16], P('cells'), may hold values 0 or 1
- courant: float32 [3, 6144], P(None, 'modes'), may hold values from 0.05 to 0.3
- upwind: int32 [3, 6144], P(None, 'modes'), may hold values from 0 to 1
- relaxation: float32 [6144], P('modes'), may hold values from 0.02 to 0.4
- source: float32 [6144], P('modes'), may hold values from -6 to 6
- coupling: bfloat16 [6144, 6144], P('modes'), may hold values from -0.0390625 to 0.0390625
Outputs:
- evolved: float32 [8, 8, 8, 16, 6144], P('cells', None, None, None, 'modes')
All inputs are finite; a program needn't handle non-finite values. No bound on the sum of `heaters` on one device may be relied on, other than what follows from the above.
Results may differ from a plain program's by a relative error of at most 0.0018.
Values may be sent and summed in bfloat16 or wider, within the bound.
A program may use at most 128 MiB of HBM per device.

v0:
```python
import jax
import jax.numpy as jnp
from jax import lax
from jax.sharding import PartitionSpec as P

GY = 4
STEPS = 2


def shifted(block, axis, distance):
    devices = range(lax.axis_size(axis))
    route = [((i - distance) % len(devices), i) for i in devices]
    return lax.ppermute(block, axis, route)


def upstream(density, forward, axis):
    widths = [(0, 0)] * density.ndim
    widths[axis] = (1, 1)
    padded = jnp.pad(density, widths)
    length_axis = density.shape[axis]
    behind = lax.slice_in_dim(padded, 0, length_axis, axis=axis)
    ahead = lax.slice_in_dim(padded, 2, length_axis + 2, axis=axis)
    return jnp.where(forward, behind, ahead)


def scatter_term(rounded, coupling):
    contract = (((1,), (1,)), ((), ()))
    gathered = lax.all_gather(rounded, "modes", axis=1, tiled=True)
    return lax.dot_general(gathered, coupling, contract, preferred_element_type=jnp.float32)


def advect(density, courant, upwind, masks):
    lower_y_ok, upper_y_ok = masks
    forward_x = upwind[0] == 1
    forward_y = upwind[1] == 1
    forward_z = upwind[2] == 1
    below_x = shifted(density[-1].astype(jnp.bfloat16), "cells", GY).astype(jnp.float32)
    above_x = shifted(density[0], "cells", -GY)
    below_y = (
        shifted(density[:, -1].astype(jnp.bfloat16), "cells", 1).astype(jnp.float32) * lower_y_ok
    )
    above_y = (
        shifted(density[:, 0].astype(jnp.bfloat16), "cells", -1).astype(jnp.float32) * upper_y_ok
    )
    upstream_z = upstream(density, forward_z, 2)
    transport = courant[0] * (density - upstream(density, forward_x, 0))
    transport = transport + courant[1] * (density - upstream(density, forward_y, 1))
    transport = transport + courant[2] * (density - upstream_z)
    transport = transport.at[0].add(-courant[0] * jnp.where(forward_x, below_x, 0.0))
    transport = transport.at[-1].add(-courant[0] * jnp.where(forward_x, 0.0, above_x))
    transport = transport.at[:, 0].add(-courant[1] * jnp.where(forward_y, below_y, 0.0))
    transport = transport.at[:, -1].add(-courant[1] * jnp.where(forward_y, 0.0, above_y))
    return transport


def per_device(phonons, heaters, courant, upwind, relaxation, source, coupling):
    density = phonons[0]
    cell_count = density.shape[0] * density.shape[1] * density.shape[2]
    mode_count = density.shape[3]
    block_total = lax.axis_size("cells")
    position = (lax.axis_index("cells") + 2) % block_total
    column = position % GY
    masks = ((column != 0).astype(jnp.float32), (column != GY - 1).astype(jnp.float32))
    heating = heaters[0].astype(jnp.float32)[..., None] * source
    for repeat in range(STEPS):
        rounded = density.astype(jnp.bfloat16).reshape(cell_count, mode_count)
        scattered = scatter_term(rounded, coupling).reshape(density.shape)
        transport = advect(density, courant, upwind, masks)
        density = density - transport - relaxation * density - scattered + heating
    return density[None]


def solution(mesh):
    placed = (
        P("cells", None, None, None, "modes"),
        P("cells", None, None, None),
        P(None, "modes"),
        P(None, "modes"),
        P("modes"),
        P("modes"),
        P("modes", None),
    )
    return jax.shard_map(
        per_device,
        mesh=mesh,
        in_specs=placed,
        out_specs=P("cells", None, None, None, "modes"),
        check_vma=False,
    )
```

profile of v0, /device:TPU:0, one launch (start us, length us, event | category | flops | bytes accessed | tf_op | source)
XLA Modules:
  0.0 519.6 jit_solution(12201974563363240435)
XLA Ops:
  6.5 5.0 convert.12
  11.6 1.0 slice_bitcast_fusion.10
  12.7 3.0 collective-permute-start
  15.7 1.2 slice_bitcast_fusion.4
  17.2 3.4 copy.37
  20.7 2.6 collective-permute-start.3
  23.5 7.2 %fusion.4 = f32[8,8,16,1536]{3,2,1,0:T(8,128)} fusion(f32[8,8,16,1536]{3,2,1,0:T(8,128)S(1)} %bitcast.82, f32[1536]{0:T(1024)S(1)} %get-tuple-element.105, f32[1536]{0:T(1024)S(1)} %get-tuple-element.106, f32[1536]{0:T(1024)S(1)} %get-tuple-element.104, pred[1536]{0:T(1024)(128)(4,1)S(1)} %get-tuple-element.102, pred[1536]{0:T(1024)(128)(4,1)S(1)} %get-tuple-element.103, ...), kind=kLoop, calls=%fused_computation.18 | loop fusion | flops 17301504 | bytes 12605952 | tf_op jit(solution)/shard_map/add | solution.py:48
  30.8 0.7 neg.21
  31.5 1.4 convert_bitcast_fusion
  32.9 2.3 fusion.35
  35.2 6.2 %copy.16 = f32[8,8,16,1536]{3,2,0,1:T(8,128)} copy(f32[8,8,16,1536]{3,2,1,0:T(8,128)} %fusion.35) | data formatting | bytes 12582912 | tf_op jit(solution)/shard_map/scatter-add | solution.py:49
  41.4 4.5 collective-permute-done.1
  45.9 2.2 fusion.34
  48.1 2.2 fusion.32
  50.3 2.1 fusion.31
  52.4 180.2 %all-gather.3.cloned.1.call-done = bf16[1024,6144]{1,0:T(8,128)(2,1)} async-done(((bf16[1024,1536]{1,0:T(8,128)(2,1)}), bf16[1024,6144]{1,0:T(8,128)(2,1)}) %all-gather.3.cloned.1.call-update) | async-done | bytes 12582928 | tf_op jit(solution)/shard_map/all_gather | solution.py:28
  232.6 24.1 %fusion.37 = f32[1024,1536]{1,0:T(8,128)S(1)} fusion(bf16[1024,6144]{1,0:T(8,128)(2,1)} %all-gather.3.cloned.1.call-done, bf16[1536,6144]{1,0:T(8,128)(2,1)} %param.29), kind=kOutput, calls=%fused_computation.77 | convolution fusion | flops 19327352832 | bytes 37748736 | tf_op jit(solution)/shard_map/dot_general | solution.py:29
  256.8 8.1 %fusion.36 = (bf16[8,8,16,1536]{3,2,1,0:T(8,128)(2,1)}, f32[8,8,16,1536]{3,2,1,0:T(8,128)}) fusion(f32[1536]{0:T(1024)S(1)} %copy-done.13, f32[8,8,16]{2,1,0:T(8,128)S(1)} %copy-done, f32[8,8,16,1536]{3,2,0,1:T(8,128)} %fusion.31, f32[8,8,16,1536]{3,2,1,0:T(8,128)S(1)} %bitcast.86, f32[1,8,8,16,1536]{4,3,2,1,0:T(8,128)} %param.23, f32[1536]{0:T(1024)S(1)} %copy-done.14), kind=kLoop, calls=%fused_computation.76 | loop fusion | flops 11010048 | bytes 28327936 | tf_op jit(solution)/shard_map/convert.2
  265.0 1.0 slice_bitcast_fusion.7
  266.0 1.5 collective-permute-start.4
  267.5 1.2 slice_bitcast_fusion.1
  269.4 18.0 %fusion.12 = f32[8,8,16,1536]{3,2,1,0:T(8,128)S(1)} fusion(f32[8,8,16,1536]{3,2,1,0:T(8,128)} %get-tuple-element.108, f32[1536]{0:T(1024)S(1)} %copy-done.12, f32[1536]{0:T(1024)S(1)} %copy-done.4, f32[1536]{0:T(1024)S(1)} %copy-done.2, pred[1536]{0:T(1024)(128)(4,1)S(1)} %copy-done.16, pred[1536]{0:T(1024)(128)(4,1)S(1)} %copy-done.7, ...), kind=kLoop, calls=%fused_computation.26 | loop fusion | flops 17301504 | bytes 12605952 | tf_op jit(solution)/shard_map/add | solution.py:48
  287.4 1.2 slice_bitcast_fusion.5
  288.8 2.6 collective-permute-start.7
  291.7 0.8 copy.20
  292.5 4.6 collective-permute-done.5
  297.2 2.1 collective-permute-done.6
  299.5 3.0 copy.22
  302.6 1.1 fusion.26
  303.6 177.9 %all-gather.5.cloned.1.call-done = bf16[1024,6144]{1,0:T(8,128)(2,1)} async-done(((bf16[1024,1536]{1,0:T(8,128)(2,1)}), bf16[1024,6144]{1,0:T(8,128)(2,1)}) %all-gather.5.cloned.1.call-update) | async-done | bytes 12582928 | tf_op jit(solution)/shard_map/all_gather | solution.py:28
  481.5 24.1 %fusion.38 = f32[1024,1536]{1,0:T(8,128)S(1)} fusion(bf16[1024,6144]{1,0:T(8,128)(2,1)} %all-gather.5.cloned.1.call-done, bf16[1536,6144]{1,0:T(8,128)(2,1)} %param.29), kind=kOutput, calls=%fused_computation.78 | convolution fusion | flops 19327352832 | bytes 37748736 | tf_op jit(solution)/shard_map/dot_general | solution.py:29
  505.6 7.1 %fusion.16 = f32[1,8,8,16,1536]{4,3,2,1,0:T(8,128)} fusion(f32[8,8,16,1536]{3,2,1,0:T(8,128)S(1)} %bitcast.85, f32[8,8,16,1536]{3,2,1,0:T(8,128)} %get-tuple-element.108, f32[8,8,16,1536]{3,2,1,0:T(8,128)} %fusion.26, f32[1536]{0:T(1024)S(1)} %copy-done.14, f32[1536]{0:T(1024)S(1)} %copy-done.13, f32[8,8,16]{2,1,0:T(8,128)S(1)} %copy-done), kind=kLoop, calls=%fused_computation.30 | loop fusion | flops 9437184 | bytes 25182208 | tf_op jit(solution)/shard_map/broadcast_in_dim | solution.py:70
  (63 shorter events, 2.1 us)
Async XLA Ops:
  6.5 226.1 %all-gather.3.cloned.1.call-start = ((), (), s32[]{:S(2)}) async-start(), calls=%async_computation | async-start | bytes 15728640 | tf_op jit(solution)/shard_map/all_gather | solution.py:28
  11.6 469.9 %all-gather.5.cloned.1.call-start = ((), (), s32[]{:S(2)}) async-start(), calls=%async_computation.1 | async-start | bytes 15728640 | tf_op jit(solution)/shard_map/all_gather | solution.py:28
  12.6 10.7 %copy-start.18 = (f32[3,1536]{1,0:T(4,128)S(1)}, f32[3,1536]{1,0:T(4,128)}, u32[]{:S(2)}) copy-start(f32[3,1536]{1,0:T(4,128)} %param.25) | copy-start | bytes 55300
  12.6 10.7 %copy-start.17 = (s32[3,1536]{1,0:T(4,128)S(1)}, s32[3,1536]{1,0:T(4,128)}, u32[]{:S(2)}) copy-start(s32[3,1536]{1,0:T(4,128)} %param.26) | copy-start | bytes 55300
  12.7 10.9 %slice-start = ((s8[6291456]{0:T(1024)(128)(4,1)}), s8[4194304]{0:T(1024)(128)(4,1)S(1)}, s32[]{:S(2)}) async-start(s8[6291456]{0:T(1024)(128)(4,1)} %bitcast.80), calls=%async_computation.2 | async-start | bytes 8388608
  12.7 20.2 %collective-permute-start = (bf16[8,16,1536]{2,1,0:T(8,128)(2,1)S(1)}, bf16[8,16,1536]{2,1,0:T(8,128)(2,1)}, u32[]{:S(2)}, u32[]{:S(2)}) collective-permute-start(bf16[8,16,1536]{2,1,0:T(8,128)(2,1)S(1)} %slice_bitcast_fusion.10), channel_id=1, source_target_pairs={{16,0},{20,4},{24,8},{28,12},{0,16},{4,20},{8,24},{12,28},{17,1},{... | collective-permute-start | bytes 1179656 | tf_op jit(solution)/shard_map/ppermute | solution.py:13
  16.9 6.6 %slice-start.1 = ((s8[6291456]{0:T(1024)(128)(4,1)}), s8[2097152]{0:T(1024)(128)(4,1)S(1)}, s32[]{:S(2)}) async-start(s8[6291456]{0:T(1024)(128)(4,1)} %bitcast.80), calls=%async_computation.3 | async-start | bytes 4194304
  16.9 29.0 %collective-permute-start.1 = (f32[8,16,1536]{2,1,0:T(8,128)S(1)}, f32[8,16,1536]{2,1,0:T(8,128)S(1)}, u32[]{:S(2)}, u32[]{:S(2)}) collective-permute-start(f32[8,16,1536]{2,1,0:T(8,128)S(1)} %slice_bitcast_fusion.4), channel_id=1, source_target_pairs={{16,0},{20,4},{24,8},{28,12},{0,16},{4,20},{8,24},{12,28},{17,1},{... | collective-permute-start | bytes 2359304 | tf_op jit(solution)/shard_map/ppermute | solution.py:13
  20.6 27.4 %collective-permute-start.2 = (bf16[8,16,1536]{2,1,0:T(8,128)(2,1)S(1)}, bf16[8,16,1536]{2,1,0:T(8,128)(2,1)S(1)}, u32[]{:S(2)}, u32[]{:S(2)}) collective-permute-start(bf16[8,16,1536]{2,1,0:T(8,128)(2,1)S(1)} %get-tuple-element.112), channel_id=1, source_target_pairs={{28,0},{0,4},{4,8},{8,12},{12,16},{16,20},{20,24},{24,28},{29,1},{... | collective-permute-start | bytes 1179656 | tf_op jit(solution)/shard_map/ppermute | solution.py:13
  20.7 29.6 %collective-permute-start.3 = (bf16[8,16,1536]{2,1,0:T(8,128)(2,1)S(1)}, bf16[8,16,1536]{2,1,0:T(8,128)(2,1)S(1)}, u32[]{:S(2)}, u32[]{:S(2)}) collective-permute-start(bf16[8,16,1536]{2,1,0:T(8,128)(2,1)S(1)} %get-tuple-element.111), channel_id=1, source_target_pairs={{4,0},{8,4},{12,8},{16,12},{20,16},{24,20},{28,24},{0,28},{5,1},{9... | collective-permute-start | bytes 1179656 | tf_op jit(solution)/shard_map/ppermute | solution.py:13
  23.4 7.4 %copy-start.3 = (f32[1536]{0:T(1024)}, f32[1536]{0:T(1024)S(1)}, u32[]{:S(2)}) copy-start(f32[1536]{0:T(1024)S(1)} %get-tuple-element.106) | copy-start | bytes 18436
  23.4 7.4 %copy-start.11 = (f32[1536]{0:T(1024)}, f32[1536]{0:T(1024)S(1)}, u32[]{:S(2)}) copy-start(f32[1536]{0:T(1024)S(1)} %get-tuple-element.105) | copy-start | bytes 18436
  23.4 7.4 %copy-start.1 = (f32[1536]{0:T(1024)}, f32[1536]{0:T(1024)S(1)}, u32[]{:S(2)}) copy-start(f32[1536]{0:T(1024)S(1)} %get-tuple-element.104) | copy-start | bytes 18436
  23.5 7.3 %copy-start.5 = (pred[1536]{0:T(1024)(128)(4,1)}, pred[1536]{0:T(1024)(128)(4,1)S(1)}, u32[]{:S(2)}) copy-start(pred[1536]{0:T(1024)(128)(4,1)S(1)} %get-tuple-element.103) | copy-start | bytes 4612
  23.5 7.3 %copy-start.8 = (pred[1536]{0:T(1024)(128)(4,1)}, pred[1536]{0:T(1024)(128)(4,1)S(1)}, u32[]{:S(2)}) copy-start(pred[1536]{0:T(1024)(128)(4,1)S(1)} %get-tuple-element.101) | copy-start | bytes 4612
  23.5 7.3 %copy-start.15 = (pred[1536]{0:T(1024)(128)(4,1)}, pred[1536]{0:T(1024)(128)(4,1)S(1)}, u32[]{:S(2)}) copy-start(pred[1536]{0:T(1024)(128)(4,1)S(1)} %get-tuple-element.102) | copy-start | bytes 4612
  35.2 10.7 %copy-start.9 = (pred[1536]{0:T(1024)(128)(4,1)S(1)}, pred[1536]{0:T(1024)(128)(4,1)}, u32[]{:S(2)}) copy-start(pred[1536]{0:T(1024)(128)(4,1)} %copy-done.8) | copy-start | bytes 4612
  35.2 12.9 %copy-start.6 = (pred[1536]{0:T(1024)(128)(4,1)S(1)}, pred[1536]{0:T(1024)(128)(4,1)}, u32[]{:S(2)}) copy-start(pred[1536]{0:T(1024)(128)(4,1)} %copy-done.5) | copy-start | bytes 4612
  52.4 204.3 %copy-start = (f32[8,8,16]{2,1,0:T(8,128)S(1)}, f32[8,8,16]{2,1,0:T(8,128)}, u32[]{:S(2)}) copy-start(f32[8,8,16]{2,1,0:T(8,128)} %convert_bitcast_fusion) | copy-start | bytes 12292
  52.4 204.3 %copy-start.13 = (f32[1536]{0:T(1024)S(1)}, f32[1536]{0:T(1024)}, u32[]{:S(2)}) copy-start(f32[1536]{0:T(1024)} %param.28) | copy-start | bytes 18436
  52.4 204.3 %copy-start.14 = (f32[1536]{0:T(1024)S(1)}, f32[1536]{0:T(1024)}, u32[]{:S(2)}) copy-start(f32[1536]{0:T(1024)} %param.27) | copy-start | bytes 18436
  256.8 12.6 %copy-start.2 = (f32[1536]{0:T(1024)S(1)}, f32[1536]{0:T(1024)}, u32[]{:S(2)}) copy-start(f32[1536]{0:T(1024)} %copy-done.1) | copy-start | bytes 18436
  256.8 12.6 %copy-start.4 = (f32[1536]{0:T(1024)S(1)}, f32[1536]{0:T(1024)}, u32[]{:S(2)}) copy-start(f32[1536]{0:T(1024)} %copy-done.3) | copy-start | bytes 18436
  256.8 12.6 %copy-start.7 = (pred[1536]{0:T(1024)(128)(4,1)S(1)}, pred[1536]{0:T(1024)(128)(4,1)}, u32[]{:S(2)}) copy-start(pred[1536]{0:T(1024)(128)(4,1)} %copy-done.5) | copy-start | bytes 4612
  256.8 12.6 %copy-start.10 = (pred[1536]{0:T(1024)(128)(4,1)S(1)}, pred[1536]{0:T(1024)(128)(4,1)}, u32[]{:S(2)}) copy-start(pred[1536]{0:T(1024)(128)(4,1)} %copy-done.8) | copy-start | bytes 4612
  256.8 12.6 %copy-start.12 = (f32[1536]{0:T(1024)S(1)}, f32[1536]{0:T(1024)}, u32[]{:S(2)}) copy-start(f32[1536]{0:T(1024)} %copy-done.11) | copy-start | bytes 18436
  256.8 12.6 %copy-start.16 = (pred[1536]{0:T(1024)(128)(4,1)S(1)}, pred[1536]{0:T(1024)(128)(4,1)}, u32[]{:S(2)}) copy-start(pred[1536]{0:T(1024)(128)(4,1)} %copy-done.15) | copy-start | bytes 4612
  266.0 25.5 %collective-permute-start.4 = (bf16[8,16,1536]{2,1,0:T(8,128)(2,1)S(1)}, bf16[8,16,1536]{2,1,0:T(8,128)(2,1)S(1)}, u32[]{:S(2)}, u32[]{:S(2)}) collective-permute-start(bf16[8,16,1536]{2,1,0:T(8,128)(2,1)S(1)} %slice_bitcast_fusion.7), channel_id=1, source_target_pairs={{16,0},{20,4},{24,8},{28,12},{0,16},{4,20},{8,24},{12,28},{17,1},{... | collective-permute-start | bytes 1179656 | tf_op jit(solution)/shard_map/ppermute | solution.py:13
  268.7 28.4 %collective-permute-start.5 = (f32[8,16,1536]{2,1,0:T(8,128)S(1)}, f32[8,16,1536]{2,1,0:T(8,128)S(1)}, u32[]{:S(2)}, u32[]{:S(2)}) collective-permute-start(f32[8,16,1536]{2,1,0:T(8,128)S(1)} %slice_bitcast_fusion.1), channel_id=1, source_target_pairs={{16,0},{20,4},{24,8},{28,12},{0,16},{4,20},{8,24},{12,28},{17,1},{... | collective-permute-start | bytes 2359304 | tf_op jit(solution)/shard_map/ppermute | solution.py:13
  288.6 10.7 %collective-permute-start.6 = (bf16[8,16,1536]{2,1,0:T(8,128)(2,1)S(1)}, bf16[8,16,1536]{2,1,0:T(8,128)(2,1)S(1)}, u32[]{:S(2)}, u32[]{:S(2)}) collective-permute-start(bf16[8,16,1536]{2,1,0:T(8,128)(2,1)S(1)} %get-tuple-element.110), channel_id=1, source_target_pairs={{28,0},{0,4},{4,8},{8,12},{12,16},{16,20},{20,24},{24,28},{29,1},{... | collective-permute-start | bytes 1179656 | tf_op jit(solution)/shard_map/ppermute | solution.py:13
  288.8 13.7 %collective-permute-start.7 = (bf16[8,16,1536]{2,1,0:T(8,128)(2,1)S(1)}, bf16[8,16,1536]{2,1,0:T(8,128)(2,1)S(1)}, u32[]{:S(2)}, u32[]{:S(2)}) collective-permute-start(bf16[8,16,1536]{2,1,0:T(8,128)(2,1)S(1)} %get-tuple-element.109), channel_id=1, source_target_pairs={{4,0},{8,4},{12,8},{16,12},{20,16},{24,20},{28,24},{0,28},{5,1},{9... | collective-permute-start | bytes 1179656 | tf_op jit(solution)/shard_map/ppermute | solution.py:13
Sparse Core Ops, SparseCore 0:
  11.7 220.8 all-gather.2
  265.1 216.3 all-gather.4
where the time goes:
time: 520 us
  waiting for transfers between devices  369 us (71%)
  other arithmetic  58.1 us (11%)
  matrix products  48.2 us (9%)
  local copies, waits for them, and re-layouts  19.2 us (4%)
  between operations  13.8 us (3%)
  starting transfers between devices  11 us (2%)
    all_gather x2, waiting for transfers between devices, scatter_term(): gathered = lax.all_gather(rounded, 'modes', axis=1, tiled=True)  358 us
    dot_general x2, matrix products, scatter_term(): lax.dot_general(gathered, coupling, contract, preferred_element_type=jnp....  48.2 us
    add x2, other arithmetic, advect(): transport = transport + courant[2] * (density - upstream_z)  25.2 us
    another operation x2, other arithmetic  13.1 us
    ppermute x8, waiting for transfers between devices, shifted(): return lax.ppermute(block, axis, route)  11.2 us
    ppermute x8, starting transfers between devices, shifted(): return lax.ppermute(block, axis, route)  11 us
  transfers between devices with their start and end apart: 10, of which 5 were waited for; matrix products, arithmetic and copies ran while one was open for 11% of the time, Pallas kernels for 0%

commit v1 on v0

--- a/solution.py
+++ b/solution.py
@@ -2,6 +2,7 @@
 import jax.numpy as jnp
 from jax import lax
 from jax.sharding import PartitionSpec as P
+from jax.lax import axis_index, axis_size, ppermute
 
 GY = 4
 STEPS = 2
@@ -24,8 +25,27 @@
 
 
 def scatter_term(rounded, coupling):
+
+    def kinds_wrap(xin, net_axis):
+        step_out = axis_index(net_axis)
+        heard = axis_size(net_axis)
+        outcome_arr, piece_now, back = (heard, step_out, xin.shape[1])
+        found = [m * outcome_arr if ii == 1 else m for ii, m in enumerate(xin.shape)]
+        g_now = jnp.zeros(found, xin.dtype)
+        dev_i = 1
+        met_up = lax.dynamic_update_slice_in_dim(g_now, xin, piece_now * back, axis=1)
+        while dev_i < outcome_arr:
+            xin = ppermute(
+                xin, net_axis, [(ii, (ii + 1) % outcome_arr) for ii in range(outcome_arr)]
+            )
+            met_up = lax.dynamic_update_slice_in_dim(
+                met_up, xin, (piece_now - dev_i) % outcome_arr * back, axis=1
+            )
+            dev_i += 1
+        return met_up
+
     contract = (((1,), (1,)), ((), ()))
-    gathered = lax.all_gather(rounded, "modes", axis=1, tiled=True)
+    gathered = kinds_wrap(rounded, net_axis="modes")
     return lax.dot_general(gathered, coupling, contract, preferred_element_type=jnp.float32)
 
 

time: 520 us -> 492 us (0.946)
  waiting for transfers between devices: 369 us -> 326 us
  local copies, waits for them, and re-layouts: 19.2 us -> 52.8 us
  between operations: 13.8 us -> 0.37 us
  other arithmetic: 58.1 us -> 48.7 us
    all_gather x2 -> x0, waiting for transfers between devices: 358 us -> none  [scatter_term(): gathered = lax.all_gather(rounded, 'modes', axis=1, tiled=True)]
    ppermute x0 -> x6, waiting for transfers between devices: none -> 323 us  [kinds_wrap(): ppermute(xin, net_axis, [(ii, (ii + 1) % outcome_arr) for ii in range(out...]
    dynamic_update_slice x0 -> x8, local copies, waits for them, and re-layouts: none -> 27.1 us  [the longest x6 21 us: kinds_wrap(): lax.dynamic_update_slice_in_dim(met_up, xin, (piece_now - dev_i) % outcom...]
    another operation x0 -> x2, local copies, waits for them, and re-layouts: none -> 12.2 us
    ppermute x8, waiting for transfers between devices: 11.2 us -> 3.39 us  [shifted(): return lax.ppermute(block, axis, route)]
  transfers between devices with their start and end apart: 10 -> 14, of which waited for: 5 -> 7; matrix products, arithmetic and copies ran while one was open for 11% -> 16% of each run, Pallas kernels for 0% -> 0%
where the time goes in v1:
time: 492 us; the launch traced here: 491 us
  waiting for transfers between devices  326 us (66%)
  local copies, waits for them, and re-layouts  52.8 us (11%)
  matrix products  50.6 us (10%)
  other arithmetic  48.7 us (10%)
  starting transfers between devices  11.8 us (2%)
    ppermute x6, waiting for transfers between devices, kinds_wrap(): ppermute(xin, net_axis, [(ii, (ii + 1) % outcome_arr) for ii in range(out...  323 us
    dot_general x2, matrix products, scatter_term(): lax.dot_general(gathered, coupling, contract, preferred_element_type=jnp....  50.6 us
    add x2, other arithmetic, advect(): transport = transport + courant[2] * (density - upstream_z)  25.5 us
    dynamic_update_slice x6, local copies, waits for them, and re-layouts, kinds_wrap(): lax.dynamic_update_slice_in_dim(met_up, xin, (piece_now - dev_i) % outcom...  21 us
    another operation x2, local copies, waits for them, and re-layouts  12.2 us
  transfers between devices with their start and end apart: 14, of which 7 were waited for; matrix products, arithmetic and copies ran while one was open for 16% of the time, Pallas kernels for 0%

profile of v1, /device:TPU:0, one launch (start us, length us, event | category | flops | bytes accessed | tf_op | source)
XLA Modules:
  0.0 490.7 jit_solution(14498961508575347192)
XLA Ops:
  0.0 3.4 convert.12
  3.4 3.1 collective-permute-start.4
  6.5 70.2 %collective-permute-done.4 = bf16[1024,1536]{1,0:T(8,128)(2,1)} collective-permute-done((bf16[1024,1536]{1,0:T(8,128)(2,1)S(1)}, bf16[1024,1536]{1,0:T(8,128)(2,1)}, u32[]{:S(2)}, u32[]{:S(2)}) %collective-permute-start.4) | collective-permute-done | bytes 3145760 | tf_op jit(solution)/shard_map/ppermute | solution.py:38
  77.5 1.5 collective-permute-start
  82.0 2.6 collective-permute-start.3
  86.5 18.3 %fusion.4 = f32[8,8,16,1536]{3,2,1,0:T(8,128)} fusion(f32[8,8,16,1536]{3,2,1,0:T(8,128)} %bitcast.80, f32[1536]{0:T(1024)S(1)} %get-tuple-element.105, f32[1536]{0:T(1024)S(1)} %get-tuple-element.106, f32[1536]{0:T(1024)S(1)} %get-tuple-element.104, pred[1536]{0:T(1024)(128)(4,1)S(1)} %get-tuple-element.102, pred[1536]{0:T(1024)(128)(4,1)S(1)} %get-tuple-element.103, ...), kind=kLoop, calls=%fused_computation.18 | loop fusion | flops 17301504 | bytes 12605952 | tf_op jit(solution)/shard_map/add | solution.py:68
  104.8 43.3 %collective-permute-done.5 = bf16[1024,1536]{1,0:T(8,128)(2,1)} collective-permute-done((bf16[1024,1536]{1,0:T(8,128)(2,1)}, bf16[1024,1536]{1,0:T(8,128)(2,1)}, u32[]{:S(2)}, u32[]{:S(2)}) %collective-permute-start.5) | collective-permute-done | bytes 3145760 | tf_op jit(solution)/shard_map/ppermute | solution.py:38
  148.1 6.1 %broadcast.148.clone = bf16[1024,6144]{1,0:T(8,128)(2,1)} broadcast(bf16[]{:T(256)} %constant.249.clone.1), dimensions={} | broadcast | bytes 12582914 | tf_op jit(solution)/shard_map/broadcast.3
  154.2 2.0 constant_dynamic-update-slice_fusion.7
  157.7 2.3 fusion.35
  160.0 3.2 copy.16
  163.3 1.5 fusion.34
  166.3 3.8 constant_dynamic-update-slice_fusion.6
  170.1 3.8 constant_dynamic-update-slice_fusion.5
  173.9 44.7 %collective-permute-done.6 = bf16[1024,1536]{1,0:T(8,128)(2,1)} collective-permute-done((bf16[1024,1536]{1,0:T(8,128)(2,1)}, bf16[1024,1536]{1,0:T(8,128)(2,1)}, u32[]{:S(2)}, u32[]{:S(2)}) %collective-permute-start.6) | collective-permute-done | bytes 3145760 | tf_op jit(solution)/shard_map/ppermute | solution.py:38
  218.6 3.9 constant_dynamic-update-slice_fusion.4
  222.6 26.5 %fusion.37 = f32[1024,1536]{1,0:T(8,128)} fusion(bf16[1024,6144]{1,0:T(8,128)(2,1)} %constant_dynamic-update-slice_fusion.4, bf16[1536,6144]{1,0:T(8,128)(2,1)} %param.29), kind=kOutput, calls=%fused_computation.85 | convolution fusion | flops 19327352832 | bytes 37748736 | tf_op jit(solution)/shard_map/dot_general | solution.py:49
  249.2 4.6 fusion.36
  253.9 69.2 %collective-permute-done.11 = bf16[1024,1536]{1,0:T(8,128)(2,1)S(1)} collective-permute-done((bf16[1024,1536]{1,0:T(8,128)(2,1)S(1)}, bf16[1024,1536]{1,0:T(8,128)(2,1)S(1)}, u32[]{:S(2)}, u32[]{:S(2)}) %collective-permute-start.11) | collective-permute-done | bytes 3145760 | tf_op jit(solution)/shard_map/ppermute | solution.py:38
  325.8 7.2 %fusion.12 = f32[8,8,16,1536]{3,2,1,0:T(8,128)} fusion(f32[8,8,16,1536]{3,2,1,0:T(8,128)S(1)} %get-tuple-element.108, f32[1536]{0:T(1024)S(1)} %copy-done.18, f32[1536]{0:T(1024)S(1)} %copy-done.10, f32[1536]{0:T(1024)S(1)} %copy-done.8, pred[1536]{0:T(1024)(128)(4,1)S(1)} %copy-done.22, pred[1536]{0:T(1024)(128)(4,1)S(1)} %copy-done.12, ...), kind=kLoop, calls=%fused_computation.26 | loop fusion | flops 17301504 | bytes 12605952 | tf_op jit(solution)/shard_map/add | solution.py:68
  333.0 58.5 %collective-permute-done.12 = bf16[1024,1536]{1,0:T(8,128)(2,1)} collective-permute-done((bf16[1024,1536]{1,0:T(8,128)(2,1)S(1)}, bf16[1024,1536]{1,0:T(8,128)(2,1)}, u32[]{:S(2)}, u32[]{:S(2)}) %collective-permute-start.12) | collective-permute-done | bytes 3145760 | tf_op jit(solution)/shard_map/ppermute | solution.py:38
  393.0 2.6 collective-permute-start.10
  395.6 6.1 %broadcast.148 = bf16[1024,6144]{1,0:T(8,128)(2,1)} broadcast(bf16[]{:T(256)} %constant.249.clone.1), dimensions={} | broadcast | bytes 12582914 | tf_op jit(solution)/shard_map/broadcast.3
  401.7 4.1 constant_dynamic-update-slice_fusion.3
  408.6 3.4 collective-permute-done.8
  413.3 1.3 fusion.27
  416.4 1.9 constant_dynamic-update-slice_fusion.2
  418.3 3.8 constant_dynamic-update-slice_fusion.1
  422.1 37.1 %collective-permute-done.13 = bf16[1024,1536]{1,0:T(8,128)(2,1)} collective-permute-done((bf16[1024,1536]{1,0:T(8,128)(2,1)}, bf16[1024,1536]{1,0:T(8,128)(2,1)}, u32[]{:S(2)}, u32[]{:S(2)}) %collective-permute-start.13) | collective-permute-done | bytes 3145760 | tf_op jit(solution)/shard_map/ppermute | solution.py:38
  459.2 3.8 constant_dynamic-update-slice_fusion
  463.0 24.1 %fusion.38 = f32[1024,1536]{1,0:T(8,128)S(1)} fusion(bf16[1024,6144]{1,0:T(8,128)(2,1)} %constant_dynamic-update-slice_fusion, bf16[1536,6144]{1,0:T(8,128)(2,1)} %param.29), kind=kOutput, calls=%fused_computation.86 | convolution fusion | flops 19327352832 | bytes 37748736 | tf_op jit(solution)/shard_map/dot_general | solution.py:49
  487.1 3.6 fusion.16
  (87 shorter events, 18.8 us)
Async XLA Ops:
  0.0 79.0 %copy-start = (f32[1,8,8,16,1536]{4,3,2,1,0:T(8,128)S(1)}, f32[1,8,8,16,1536]{4,3,2,1,0:T(8,128)}, u32[]{:S(2)}) copy-start(f32[1,8,8,16,1536]{4,3,2,1,0:T(8,128)} %param.23) | copy-start | bytes 18874372
  3.4 73.3 %collective-permute-start.4 = (bf16[1024,1536]{1,0:T(8,128)(2,1)S(1)}, bf16[1024,1536]{1,0:T(8,128)(2,1)}, u32[]{:S(2)}, u32[]{:S(2)}) collective-permute-start(bf16[1024,1536]{1,0:T(8,128)(2,1)S(1)} %bitcast.85), channel_id=1, source_target_pairs={{0,1},{1,2},{2,3},{3,0},{4,5},{5,6},{6,7},{7,4},{8,9},{9,10},{10,1... | collective-permute-start | bytes 9437192 | tf_op jit(solution)/shard_map/ppermute | solution.py:38
  76.7 71.4 %collective-permute-start.5 = (bf16[1024,1536]{1,0:T(8,128)(2,1)}, bf16[1024,1536]{1,0:T(8,128)(2,1)}, u32[]{:S(2)}, u32[]{:S(2)}) collective-permute-start(bf16[1024,1536]{1,0:T(8,128)(2,1)} %collective-permute-done.4), channel_id=1, source_target_pairs={{0,1},{1,2},{2,3},{3,0},{4,5},{5,6},{6,7},{7,4},{8,9},{9,10},{10,1... | collective-permute-start | bytes 9437192 | tf_op jit(solution)/shard_map/ppermute | solution.py:38
  77.5 80.2 %collective-permute-start = (bf16[8,16,1536]{2,1,0:T(8,128)(2,1)}, bf16[8,16,1536]{2,1,0:T(8,128)(2,1)}, u32[]{:S(2)}, u32[]{:S(2)}) collective-permute-start(bf16[8,16,1536]{2,1,0:T(8,128)(2,1)} %slice_bitcast_fusion.10), channel_id=1, source_target_pairs={{16,0},{20,4},{24,8},{28,12},{0,16},{4,20},{8,24},{12,28},{17,1},{... | collective-permute-start | bytes 1179656 | tf_op jit(solution)/shard_map/ppermute | solution.py:14
  80.0 83.3 %collective-permute-start.1 = (f32[8,16,1536]{2,1,0:T(8,128)}, f32[8,16,1536]{2,1,0:T(8,128)}, u32[]{:S(2)}, u32[]{:S(2)}) collective-permute-start(f32[8,16,1536]{2,1,0:T(8,128)} %slice_bitcast_fusion.4), channel_id=1, source_target_pairs={{16,0},{20,4},{24,8},{28,12},{0,16},{4,20},{8,24},{12,28},{17,1},{... | collective-permute-start | bytes 2359304 | tf_op jit(solution)/shard_map/ppermute | solution.py:14
  82.0 82.8 %collective-permute-start.2 = (bf16[8,16,1536]{2,1,0:T(8,128)(2,1)}, bf16[8,16,1536]{2,1,0:T(8,128)(2,1)}, u32[]{:S(2)}, u32[]{:S(2)}) collective-permute-start(bf16[8,16,1536]{2,1,0:T(8,128)(2,1)} %get-tuple-element.112), channel_id=1, source_target_pairs={{28,0},{0,4},{4,8},{8,12},{12,16},{16,20},{20,24},{24,28},{29,1},{... | collective-permute-start | bytes 1179656 | tf_op jit(solution)/shard_map/ppermute | solution.py:14
  82.0 84.1 %collective-permute-start.3 = (bf16[8,16,1536]{2,1,0:T(8,128)(2,1)}, bf16[8,16,1536]{2,1,0:T(8,128)(2,1)S(1)}, u32[]{:S(2)}, u32[]{:S(2)}) collective-permute-start(bf16[8,16,1536]{2,1,0:T(8,128)(2,1)} %get-tuple-element.111), channel_id=1, source_target_pairs={{4,0},{8,4},{12,8},{16,12},{20,16},{24,20},{28,24},{0,28},{5,1},{9... | collective-permute-start | bytes 1179656 | tf_op jit(solution)/shard_map/ppermute | solution.py:14
  85.5 19.3 %copy-start.9 = (f32[1536]{0:T(1024)}, f32[1536]{0:T(1024)S(1)}, u32[]{:S(2)}) copy-start(f32[1536]{0:T(1024)S(1)} %get-tuple-element.106) | copy-start | bytes 18436
  85.5 19.3 %copy-start.17 = (f32[1536]{0:T(1024)}, f32[1536]{0:T(1024)S(1)}, u32[]{:S(2)}) copy-start(f32[1536]{0:T(1024)S(1)} %get-tuple-element.105) | copy-start | bytes 18436
  85.5 70.7 %copy-start.7 = (f32[1536]{0:T(1024)}, f32[1536]{0:T(1024)S(1)}, u32[]{:S(2)}) copy-start(f32[1536]{0:T(1024)S(1)} %get-tuple-element.104) | copy-start | bytes 18436
  86.5 18.3 %copy-start.11 = (pred[1536]{0:T(1024)(128)(4,1)}, pred[1536]{0:T(1024)(128)(4,1)S(1)}, u32[]{:S(2)}) copy-start(pred[1536]{0:T(1024)(128)(4,1)S(1)} %get-tuple-element.103) | copy-start | bytes 4612
  86.5 18.3 %copy-start.14 = (pred[1536]{0:T(1024)(128)(4,1)}, pred[1536]{0:T(1024)(128)(4,1)S(1)}, u32[]{:S(2)}) copy-start(pred[1536]{0:T(1024)(128)(4,1)S(1)} %get-tuple-element.101) | copy-start | bytes 4612
  86.5 18.3 %copy-start.21 = (pred[1536]{0:T(1024)(128)(4,1)}, pred[1536]{0:T(1024)(128)(4,1)S(1)}, u32[]{:S(2)}) copy-start(pred[1536]{0:T(1024)(128)(4,1)S(1)} %get-tuple-element.102) | copy-start | bytes 4612
  148.1 70.5 %collective-permute-start.6 = (bf16[1024,1536]{1,0:T(8,128)(2,1)}, bf16[1024,1536]{1,0:T(8,128)(2,1)}, u32[]{:S(2)}, u32[]{:S(2)}) collective-permute-start(bf16[1024,1536]{1,0:T(8,128)(2,1)} %collective-permute-done.5), channel_id=1, source_target_pairs={{0,1},{1,2},{2,3},{3,0},{4,5},{5,6},{6,7},{7,4},{8,9},{9,10},{10,1... | collective-permute-start | bytes 9437192 | tf_op jit(solution)/shard_map/ppermute | solution.py:38
  157.7 91.4 %copy-start.5 = (f32[8,8,16]{2,1,0:T(8,128)}, f32[8,8,16]{2,1,0:T(8,128)S(1)}, u32[]{:S(2)}) copy-start(f32[8,8,16]{2,1,0:T(8,128)S(1)} %convert_bitcast_fusion) | copy-start | bytes 12292
  218.6 30.5 %slice-start = ((s8[6291456]{0:T(1024)(128)(4,1)}), s8[4194304]{0:T(1024)(128)(4,1)S(1)}, s32[]{:S(2)}) async-start(s8[6291456]{0:T(1024)(128)(4,1)} %bitcast.81), calls=%async_computation | async-start | bytes 8388608
  222.6 26.6 %slice-start.1 = ((s8[6291456]{0:T(1024)(128)(4,1)}), s8[2097152]{0:T(1024)(128)(4,1)S(1)}, s32[]{:S(2)}) async-start(s8[6291456]{0:T(1024)(128)(4,1)} %bitcast.81), calls=%async_computation.1 | async-start | bytes 4194304
  222.6 26.6 %copy-start.19 = (f32[1536]{0:T(1024)S(1)}, f32[1536]{0:T(1024)}, u32[]{:S(2)}) copy-start(f32[1536]{0:T(1024)} %param.28) | copy-start | bytes 18436
  222.6 26.6 %copy-start.20 = (f32[1536]{0:T(1024)S(1)}, f32[1536]{0:T(1024)}, u32[]{:S(2)}) copy-start(f32[1536]{0:T(1024)} %param.27) | copy-start | bytes 18436
  249.1 76.6 %copy-start.8 = (f32[1536]{0:T(1024)S(1)}, f32[1536]{0:T(1024)}, u32[]{:S(2)}) copy-start(f32[1536]{0:T(1024)} %copy-done.7) | copy-start | bytes 18436
  249.2 76.6 %copy-start.10 = (f32[1536]{0:T(1024)S(1)}, f32[1536]{0:T(1024)}, u32[]{:S(2)}) copy-start(f32[1536]{0:T(1024)} %copy-done.9) | copy-start | bytes 18436
  249.2 76.6 %copy-start.18 = (f32[1536]{0:T(1024)S(1)}, f32[1536]{0:T(1024)}, u32[]{:S(2)}) copy-start(f32[1536]{0:T(1024)} %copy-done.17) | copy-start | bytes 18436
  249.2 76.6 %copy-start.22 = (pred[1536]{0:T(1024)(128)(4,1)S(1)}, pred[1536]{0:T(1024)(128)(4,1)}, u32[]{:S(2)}) copy-start(pred[1536]{0:T(1024)(128)(4,1)} %copy-done.21) | copy-start | bytes 4612
  253.8 137.7 %copy-start.2 = (bf16[8,8,16,1536]{3,2,1,0:T(8,128)(2,1)}, bf16[8,8,16,1536]{3,2,1,0:T(8,128)(2,1)S(1)}, u32[]{:S(2)}) copy-start(bf16[8,8,16,1536]{3,2,1,0:T(8,128)(2,1)S(1)} %get-tuple-element.107) | copy-start | bytes 9437188
  253.8 69.3 %collective-permute-start.11 = (bf16[1024,1536]{1,0:T(8,128)(2,1)S(1)}, bf16[1024,1536]{1,0:T(8,128)(2,1)S(1)}, u32[]{:S(2)}, u32[]{:S(2)}) collective-permute-start(bf16[1024,1536]{1,0:T(8,128)(2,1)S(1)} %bitcast.83), channel_id=1, source_target_pairs={{0,1},{1,2},{2,3},{3,0},{4,5},{5,6},{6,7},{7,4},{8,9},{9,10},{10,1... | collective-permute-start | bytes 9437192 | tf_op jit(solution)/shard_map/ppermute | solution.py:38
  323.1 68.4 %collective-permute-start.12 = (bf16[1024,1536]{1,0:T(8,128)(2,1)S(1)}, bf16[1024,1536]{1,0:T(8,128)(2,1)}, u32[]{:S(2)}, u32[]{:S(2)}) collective-permute-start(bf16[1024,1536]{1,0:T(8,128)(2,1)S(1)} %collective-permute-done.11), channel_id=1, source_target_pairs={{0,1},{1,2},{2,3},{3,0},{4,5},{5,6},{6,7},{7,4},{8,9},{9,10},{10,1... | collective-permute-start | bytes 9437192 | tf_op jit(solution)/shard_map/ppermute | solution.py:38
  323.9 81.8 %collective-permute-start.7 = (bf16[8,16,1536]{2,1,0:T(8,128)(2,1)}, bf16[8,16,1536]{2,1,0:T(8,128)(2,1)}, u32[]{:S(2)}, u32[]{:S(2)}) collective-permute-start(bf16[8,16,1536]{2,1,0:T(8,128)(2,1)} %slice_bitcast_fusion.7), channel_id=1, source_target_pairs={{16,0},{20,4},{24,8},{28,12},{0,16},{4,20},{8,24},{12,28},{17,1},{... | collective-permute-start | bytes 1179656 | tf_op jit(solution)/shard_map/ppermute | solution.py:14
  391.5 67.7 %collective-permute-start.13 = (bf16[1024,1536]{1,0:T(8,128)(2,1)}, bf16[1024,1536]{1,0:T(8,128)(2,1)}, u32[]{:S(2)}, u32[]{:S(2)}) collective-permute-start(bf16[1024,1536]{1,0:T(8,128)(2,1)} %collective-permute-done.12), channel_id=1, source_target_pairs={{0,1},{1,2},{2,3},{3,0},{4,5},{5,6},{6,7},{7,4},{8,9},{9,10},{10,1... | collective-permute-start | bytes 9437192 | tf_op jit(solution)/shard_map/ppermute | solution.py:38
  392.4 19.6 %collective-permute-start.8 = (f32[8,16,1536]{2,1,0:T(8,128)}, f32[8,16,1536]{2,1,0:T(8,128)}, u32[]{:S(2)}, u32[]{:S(2)}) collective-permute-start(f32[8,16,1536]{2,1,0:T(8,128)} %slice_bitcast_fusion.1), channel_id=1, source_target_pairs={{16,0},{20,4},{24,8},{28,12},{0,16},{4,20},{8,24},{12,28},{17,1},{... | collective-permute-start | bytes 2359304 | tf_op jit(solution)/shard_map/ppermute | solution.py:14
  393.0 20.3 %collective-permute-start.9 = (bf16[8,16,1536]{2,1,0:T(8,128)(2,1)}, bf16[8,16,1536]{2,1,0:T(8,128)(2,1)}, u32[]{:S(2)}, u32[]{:S(2)}) collective-permute-start(bf16[8,16,1536]{2,1,0:T(8,128)(2,1)} %get-tuple-element.110), channel_id=1, source_target_pairs={{28,0},{0,4},{4,8},{8,12},{12,16},{16,20},{20,24},{24,28},{29,1},{... | collective-permute-start | bytes 1179656 | tf_op jit(solution)/shard_map/ppermute | solution.py:14
  393.0 22.1 %collective-permute-start.10 = (bf16[8,16,1536]{2,1,0:T(8,128)(2,1)}, bf16[8,16,1536]{2,1,0:T(8,128)(2,1)S(1)}, u32[]{:S(2)}, u32[]{:S(2)}) collective-permute-start(bf16[8,16,1536]{2,1,0:T(8,128)(2,1)} %get-tuple-element.109), channel_id=1, source_target_pairs={{4,0},{8,4},{12,8},{16,12},{20,16},{24,20},{28,24},{0,28},{5,1},{9... | collective-permute-start | bytes 1179656 | tf_op jit(solution)/shard_map/ppermute | solution.py:14
  463.0 24.1 %copy-start.6 = (f32[8,8,16]{2,1,0:T(8,128)S(1)}, f32[8,8,16]{2,1,0:T(8,128)}, u32[]{:S(2)}) copy-start(f32[8,8,16]{2,1,0:T(8,128)} %copy-done.5) | copy-start | bytes 12292
  (7 other events, 40.3 us)
